TPU v7x, 256 devices: a whole 4x4x8 slice. The times are simulated.
256 devices in a mesh: section: 4 (over z_lo, core), expert: 64 (over z_hi, y, x).
Axes of the slice: x: 4, y: 4, z: 8 (z_hi: 4, z_lo: 2; z = z_hi * 2 + z_lo), core: 2. Of those that a mesh axis runs over, the one named last changes fastest.
Arguments:
- grad_out: bfloat16 [4, 8192, 3584], P('section', 'expert'), may hold values from -6 to 6
- expert_ids: int32 [4, 8192, 8], P('section', 'expert'), may hold values from 0 to 63, all different within a row; in each aligned block of 128 rows (0 to 127, 128 to 255, ..., all dimensions but the last counted through in order) at most 20 rows name the same one
- gate_weights: bfloat16 [4, 8192, 8], P('section', 'expert'), may hold values from 0.019897461 to 0.5
- down_weight: bfloat16 [4, 64, 1024, 3584], P('section', 'expert'), may hold values from -0.09375 to 0.09375
- hidden_saved: bfloat16 [4, 64, 64, 20, 1024], P('section', 'expert'), may hold values from -0.19921875 to 0.19921875
Outputs:
- hidden_grad: bfloat16 [4, 64, 64, 20, 1024], P('section', 'expert')
- gate_grad: float32 [4, 8192, 8], P('section', 'expert')
Inputs may be any that keep to these rules, and one draw needn't show every extreme that they name: `expert_ids`: each token names 8 distinct experts; among the tokens of one index of expert in one section, no expert is named by more than 20 of them, a bound that some block reaches.
All inputs are finite; a program needn't handle non-finite values.
Results may differ from a plain program's by a relative error of at most 0.001.
Values may be sent and summed in bfloat16 or wider, within the bound.
No kernel may reach another device: no remote copies, remote signals or barrier semaphores. Data moves between devices by JAX's collectives and lax.ppermute only.
A program may use at most 128 MiB of HBM per device.

v0:
```python
import jax
import jax.numpy as jnp
from jax import lax
from jax.sharding import PartitionSpec as P


def shifted(x, axis, by):
    size = lax.axis_size(axis)
    return lax.ppermute(x, axis, [(i, (i + by) % size) for i in range(size)])


def slot_places(ids_local, experts, most):
    flat = ids_local.reshape(-1)
    onehot = (flat[:, None] == jnp.arange(experts, dtype=jnp.int32)[None, :]).astype(jnp.int32)
    rank = jnp.sum(jnp.cumsum(onehot, 0) * onehot, 1) - 1
    return flat * most + rank


def pack_rows(grad_local, dest, experts, most, top_count):
    token = jnp.arange(dest.shape[0], dtype=jnp.int32) // top_count
    rows = (
        jnp.zeros((experts * most, grad_local.shape[1]), jnp.bfloat16)
        .at[dest]
        .set(grad_local[token])
    )
    return rows.reshape(experts, most, grad_local.shape[1])


def pack_gates(gates_local, dest, experts, most):
    weights = jnp.zeros((experts * most,), jnp.bfloat16).at[dest].set(gates_local.reshape(-1))
    return weights.reshape(experts, most)


def project_back(rows_in, weight_part):
    flat_rows = rows_in.reshape(-1, rows_in.shape[2])
    return lax.dot_general(
        flat_rows, weight_part, (((1,), (1,)), ((), ())), preferred_element_type=jnp.float32
    )


def local(grad_out, expert_ids, gate_weights, down_weight, hidden_saved):
    experts = lax.axis_size("expert")
    most = hidden_saved.shape[3]
    hidden_width = down_weight.shape[2]
    top_count = expert_ids.shape[2]
    dest = slot_places(expert_ids[0], experts, most)
    gate_buf = pack_gates(gate_weights[0], dest, experts, most)
    incoming = shifted(grad_out[0], "section", -1)
    rows_buf = pack_rows(incoming, dest, experts, most, top_count)
    rows_in, gates_in = (
        lax.all_to_all(rows_buf, "expert", split_axis=0, concat_axis=0, tiled=True),
        lax.all_to_all(gate_buf, "expert", split_axis=0, concat_axis=0, tiled=True),
    )
    back = project_back(rows_in, down_weight[0, 0])
    hidden_grad = (gates_in.reshape(-1).astype(jnp.float32)[:, None] * back).astype(jnp.bfloat16)
    saved = hidden_saved[0, 0].reshape(experts * most, hidden_width)
    slot_grad = jnp.sum(saved.astype(jnp.float32) * back, axis=1).reshape(experts, most)
    returned = lax.all_to_all(slot_grad, "expert", split_axis=0, concat_axis=0, tiled=True)
    gate_grad = returned.reshape(-1)[dest].reshape(1, expert_ids.shape[1], top_count)
    return (hidden_grad.reshape(1, 1, experts, most, hidden_width), gate_grad)


def solution(mesh):
    in_specs = (
        P("section", "expert", None),
        P("section", "expert", None),
        P("section", "expert", None),
        P("section", "expert", None, None),
        P("section", "expert", None, None, None),
    )
    out_specs = (P("section", "expert", None, None, None), P("section", "expert", None))
    return jax.shard_map(local, mesh=mesh, in_specs=in_specs, out_specs=out_specs, check_vma=False)
```

profile of v0, /device:TPU:2, one launch (start us, length us, event | category | flops | bytes accessed | tf_op | source)
XLA Modules:
  0.0 431.6 jit_solution(11115676847194136063)
XLA Ops:
  0.6 1.4 collective-permute-start
  2.1 0.8 copy.19
  2.8 0.1 eq.29
  3.0 18.0 %reduce-window.6 = s32[64,8,128]{2,1,0:T(8,128)S(1)} reduce-window(s32[64,8,128]{2,1,0:T(8,128)S(1)} %fusion.7, s32[]{:T(128)} %constant.29.clone.1), window={size=1x1x128 pad=0_0x0_0x127_0}, to_apply=%region_0.0 | reduce-window | flops 8323072 | bytes 524292 | tf_op jit(solution)/shard_map/reduce-window
  21.0 0.1 slice.12
  21.1 0.1 copy.21
  21.3 0.1 copy.22
  21.4 0.1 broadcast_add_fusion
  21.5 0.7 broadcast_multiply_fusion
  22.2 0.1 eq.25
  22.3 0.1 copy.18
  22.4 0.1 mul.32
  22.5 0.8 copy.23
  23.3 0.1 reshape.160
  23.4 0.1 fusion.6
  23.5 7.6 %scatter_custom_fusion = bf16[1280]{0:T(1024)(128)(2,1)S(1)} fusion(s32[1024]{0:T(1024)S(1)} %bitcast.27, bf16[1024]{0:T(1024)(128)(2,1)S(1)} %reshape.160, bf16[]{:T(256)} %constant.27.clone.1), kind=kCustom, calls=%fused_computation.29 | custom fusion | bytes 2562 | tf_op jit(solution)/shard_map/scatter | solution.py:30
  31.1 0.7 all_to_all.20
  31.8 13.7 %all-to-all-start = ((bf16[64,1,20]{2,1,0:T(2,128)(2,1)}), bf16[64,1,20]{2,1,0:T(2,128)(2,1)S(1)}, u32[]{:S(2)}, u32[]{:S(2)}) async-start(bf16[64,1,20]{2,1,0:T(2,128)(2,1)} %all_to_all.20), calls=%async_computation | async-start | bytes 65536 | tf_op jit(solution)/shard_map/all_to_all | solution.py:52
  45.6 0.0 collective-permute-done
  45.6 46.8 %scatter_custom_fusion.1 = bf16[1280,3584]{1,0:T(8,128)(2,1)} fusion(s32[1024]{0:T(1024)S(1)} %bitcast.28, bf16[128,3584]{1,0:T(8,128)(2,1)S(1)} %collective-permute-done, s32[1024]{0:T(1024)S(1)} %broadcast_clamp_fusion.1, bf16[]{:T(256)} %constant.27.clone.1), kind=kCustom, calls=%fused_computation.6 | custom fusion | bytes 9175042 | tf_op jit(solution)/shard_map/scatter | solution.py:24
  92.5 13.1 %reshape.133 = bf16[64,20,3584]{2,1,0:T(8,128)(2,1)} reshape(bf16[1280,3584]{1,0:T(8,128)(2,1)} %scatter_custom_fusion.1) | data formatting | bytes 18350080 | tf_op jit(solution)/shard_map/reshape | solution.py:26
  105.6 0.0 copy-start
  105.6 0.0 all-to-all-done
  105.6 13.0 %all-to-all-start.1 = ((bf16[64,20,3584]{2,1,0:T(8,128)(2,1)}), bf16[64,20,3584]{2,1,0:T(8,128)(2,1)}, u32[]{:S(2)}, u32[]{:S(2)}) async-start(bf16[64,20,3584]{2,1,0:T(8,128)(2,1)} %reshape.133), calls=%async_computation.1 | async-start | bytes 22020096 | tf_op jit(solution)/shard_map/all_to_all | solution.py:51
  118.7 0.0 copy-done
  118.7 4.3 copy.25
  122.9 6.8 %reshape.139 = f32[1280,1024]{1,0:T(8,128)} reshape(f32[1,1,64,20,1024]{4,3,2,1,0:T(8,128)} %copy.25) | data formatting | bytes 10485760 | tf_op jit(solution)/shard_map/convert_element_type | solution.py:57
  129.7 0.1 convert_reduce_fusion
  129.8 0.1 reshape.138
  129.9 230.8 %all-to-all-done.1 = bf16[64,20,3584]{2,1,0:T(8,128)(2,1)} async-done(((bf16[64,20,3584]{2,1,0:T(8,128)(2,1)}), bf16[64,20,3584]{2,1,0:T(8,128)(2,1)}, u32[]{:S(2)}, u32[]{:S(2)}) %all-to-all-start.1) | async-done | bytes 9175072 | tf_op jit(solution)/shard_map/all_to_all | solution.py:51
  360.7 13.2 %reshape.134 = bf16[1280,3584]{1,0:T(8,128)(2,1)} reshape(bf16[64,20,3584]{2,1,0:T(8,128)(2,1)} %all-to-all-done.1) | data formatting | bytes 18350080 | tf_op jit(solution)/shard_map/reshape | solution.py:35
  373.9 16.3 %multiply_reduce_fusion = (f32[1280]{0:T(1024)S(1)}, bf16[1280,1024]{1,0:T(8,128)(2,1)}) fusion(f32[1280,1024]{1,0:T(8,128)} %reshape.139, f32[1280]{0:T(1024)S(1)} %reshape.138, bf16[1280,3584]{1,0:T(8,128)(2,1)} %reshape.134, bf16[1,1,1024,3584]{3,2,1,0:T(8,128)(2,1)} %param.8), kind=kOutput, calls=%fused_computation.8 | convolution fusion | flops 9400482816 | bytes 24389632 | tf_op jit(solution)/shard_map/dot_general | solution.py:36
  390.2 0.7 all_to_all.18
  390.9 21.3 %all-to-all-start.2 = ((f32[64,1,20]{2,1,0:T(1,128)}), f32[64,1,20]{2,1,0:T(1,128)S(1)}, u32[]{:S(2)}, u32[]{:S(2)}) async-start(f32[64,1,20]{2,1,0:T(1,128)} %bitcast.7), calls=%async_computation.2 | async-start | bytes 65536 | tf_op jit(solution)/shard_map/all_to_all | solution.py:58
  412.2 3.5 reshape.135
  415.8 2.9 copy.27
  418.7 4.4 %all-to-all-done.2 = f32[64,1,20]{2,1,0:T(1,128)S(1)} async-done(((f32[64,1,20]{2,1,0:T(1,128)}), f32[64,1,20]{2,1,0:T(1,128)S(1)}, u32[]{:S(2)}, u32[]{:S(2)}) %all-to-all-start.2) | async-done | bytes 5152 | tf_op jit(solution)/shard_map/all_to_all | solution.py:58
  423.1 0.5 broadcast.142
  423.6 0.7 reduce.7
  424.4 0.1 reshape.136
  424.5 6.2 %gather_fusion = f32[1024]{0:T(1024)S(1)} fusion(f32[1280]{0:T(1024)S(1)} %reshape.136, s32[1024]{0:T(1024)S(1)} %broadcast_clamp_fusion), kind=kCustom, calls=%fused_computation.1 | custom fusion | bytes 12288 | tf_op jit(solution)/shard_map/gather | solution.py:59
  430.6 0.1 reshape.137
  430.7 0.7 copy.28
  (8 shorter events, 0.1 us)
Async XLA Ops:
  0.6 45.0 %collective-permute-start = (bf16[128,3584]{1,0:T(8,128)(2,1)}, bf16[128,3584]{1,0:T(8,128)(2,1)S(1)}, u32[]{:S(2)}, u32[]{:S(2)}) collective-permute-start(bf16[128,3584]{1,0:T(8,128)(2,1)} %bitcast.32), channel_id=1, source_target_pairs={{0,192},{64,0},{128,64},{192,128},{1,193},{65,1},{129,65},{193,129... | collective-permute-start | bytes 2752520 | tf_op jit(solution)/shard_map/ppermute | solution.py:9
  31.8 73.8 %all-to-all-start = ((bf16[64,1,20]{2,1,0:T(2,128)(2,1)}), bf16[64,1,20]{2,1,0:T(2,128)(2,1)S(1)}, u32[]{:S(2)}, u32[]{:S(2)}) async-start(bf16[64,1,20]{2,1,0:T(2,128)(2,1)} %all_to_all.20), calls=%async_computation | async-start | bytes 65536 | tf_op jit(solution)/shard_map/all_to_all | solution.py:52
  105.6 13.1 %copy-start = (bf16[1,1,64,20,1024]{4,2,3,1,0:T(8,128)(2,1)S(1)}, bf16[1,1,64,20,1024]{4,2,3,1,0:T(8,128)(2,1)}, u32[]{:S(2)}) copy-start(bf16[1,1,64,20,1024]{4,2,3,1,0:T(8,128)(2,1)} %param.9) | copy-start | bytes 7864324
  105.6 255.1 %all-to-all-start.1 = ((bf16[64,20,3584]{2,1,0:T(8,128)(2,1)}), bf16[64,20,3584]{2,1,0:T(8,128)(2,1)}, u32[]{:S(2)}, u32[]{:S(2)}) async-start(bf16[64,20,3584]{2,1,0:T(8,128)(2,1)} %reshape.133), calls=%async_computation.1 | async-start | bytes 22020096 | tf_op jit(solution)/shard_map/all_to_all | solution.py:51
  390.9 32.2 %all-to-all-start.2 = ((f32[64,1,20]{2,1,0:T(1,128)}), f32[64,1,20]{2,1,0:T(1,128)S(1)}, u32[]{:S(2)}, u32[]{:S(2)}) async-start(f32[64,1,20]{2,1,0:T(1,128)} %bitcast.7), calls=%async_computation.2 | async-start | bytes 65536 | tf_op jit(solution)/shard_map/all_to_all | solution.py:58
where the time goes:
time: 439 us; the launch traced here: 432 us
  waiting for transfers between devices  235 us (54%)
  local copies, waits for them, and re-layouts  110 us (25%)
  starting transfers between devices  49.5 us (11%)
  other arithmetic  19.8 us (5%)
  matrix products  16.3 us (4%)
    all_to_all x1, waiting for transfers between devices, local(): lax.all_to_all(rows_buf, 'expert', split_axis=0, concat_axis=0, tiled=True)  231 us
    scatter x1, local copies, waits for them, and re-layouts, pack_rows(): rows = jnp.zeros((experts * most, grad_local.shape[1]), jnp.bfloat16).at[...  46.8 us
    all_to_all x1, starting transfers between devices, local(): lax.all_to_all(slot_grad, 'expert', split_axis=0, concat_axis=0, tiled=True)  21.3 us
    another operation x3, other arithmetic  18.2 us
    dot_general x1, matrix products, project_back(): lax.dot_general(flat_rows, weight_part, (((1,), (1,)), ((), ())), preferr...  16.3 us
    all_to_all x1, starting transfers between devices, local(): lax.all_to_all(gate_buf, 'expert', split_axis=0, concat_axis=0, tiled=True)  13.7 us
    reshape x1, local copies, waits for them, and re-layouts, project_back(): flat_rows = rows_in.reshape(-1, rows_in.shape[2])  13.2 us
    reshape x1, local copies, waits for them, and re-layouts, pack_rows(): return rows.reshape(experts, most, grad_local.shape[1])  13.1 us
  transfers between devices with their start and end apart: 4, of which 2 were waited for; matrix products, arithmetic and copies ran while one was open for 25% of the time, Pallas kernels for 0%

commit v1 on v0

v1 whole, which is shorter than its diff:
```python
import functools

import jax
import jax.numpy as jnp
from jax import lax
from jax.experimental import pallas as pl
from jax.experimental.pallas import tpu as pltpu
from jax.sharding import Mesh
from jax.sharding import PartitionSpec as P

RING = 4
MAIN = 16
F32 = jnp.float32
BF16 = jnp.bfloat16
HIGH = lax.Precision.HIGHEST


def iota(shape, dim):
    return lax.broadcasted_iota(jnp.int32, shape, dim)


def ranks_of(ids, experts):
    match = jnp.zeros(experts.shape, F32)
    for k in range(ids.shape[0]):
        match = jnp.where(ids[k : k + 1, :] == experts, 1.0, match)
    tokens = ids.shape[1]
    before = jnp.where(iota((tokens, tokens), 0) < iota((tokens, tokens), 1), 1.0, 0.0).astype(BF16)
    rank = jnp.dot(match.astype(BF16), before, preferred_element_type=F32)
    return jnp.where(match > 0.5, rank, -1.0)


def spread(rank, rows_per):
    n, total = rank.shape[0], rank.shape[0] * rows_per
    pick = jnp.where(iota((total, n), 0) // rows_per == iota((total, n), 1), 1.0, 0.0).astype(BF16)
    return jnp.dot(pick, rank.astype(BF16), preferred_element_type=F32)


def own_index_kernel(ring_ref, meta_ref, rank_ref, pick_ref):
    top = meta_ref.shape[0] // 2
    experts, tokens = rank_ref.shape
    plane = experts // RING
    ids = meta_ref[0:top, :].astype(F32)
    rank_ref[...] = ranks_of(ids, iota((experts, tokens), 0).astype(F32))
    first = ring_ref[0] * plane
    rank = ranks_of(ids, (iota((plane, tokens), 0) + first).astype(F32))
    rows = plane * MAIN
    slot = (iota((rows, tokens), 0) % MAIN).astype(F32)
    pick_ref[...] = jnp.where(spread(rank, MAIN) == slot, 1.0, 0.0).astype(BF16)


def index_kernel(most, ring_ref, m0_ref, m1_ref, m2_ref, m3_ref, side_ref, far_ref, rest_ref, weight_ref):
    top = m0_ref.shape[0] // 2
    tokens = m0_ref.shape[1]
    plane = far_ref.shape[0] // MAIN
    lanes = weight_ref.shape[1]
    experts = (iota((plane, tokens), 0) + ring_ref[0] * plane).astype(F32)
    ranks, weights = [], None
    for j, ref in enumerate((m0_ref, m1_ref, m2_ref, m3_ref)):
        meta = ref[...].astype(F32)
        ids, gates = meta[0:top, :], meta[top : 2 * top, :]
        rank = ranks_of(ids, experts)
        ranks.append(rank)
        gate = jnp.zeros((plane, tokens), F32)
        for k in range(top):
            gate = jnp.where(ids[k : k + 1, :] == experts, gates[k : k + 1, :], gate)
        slots = jnp.zeros((plane, lanes), F32)
        for r in range(most):
            column = jnp.sum(jnp.where(rank == float(r), gate, 0.0), axis=1, keepdims=True)
            slots = jnp.where(iota((plane, lanes), 1) == r, column, slots)
        place = iota((plane * 8, plane), 0) == iota((plane * 8, plane), 1) * 8 + j
        placed = jnp.dot(
            jnp.where(place, 1.0, 0.0).astype(BF16), slots.astype(BF16), preferred_element_type=F32
        )
        weights = placed if weights is None else weights + placed
    weight_ref[...] = weights.astype(BF16)

    rows = plane * MAIN
    slot = (iota((rows, tokens), 0) % MAIN).astype(F32)
    far_ref[...] = jnp.where(spread(ranks[2], MAIN) == slot, 1.0, 0.0).astype(BF16)

    row = iota((2 * rows, tokens), 0)
    slot = (row % MAIN).astype(F32)
    for side, j in enumerate((1, 3)):
        keep = (spread(ranks[j], 2 * MAIN) == slot) & ((row // MAIN) % 2 == side)
        side_ref[:, side * tokens : (side + 1) * tokens] = jnp.where(keep, 1.0, 0.0).astype(BF16)

    extra = most - MAIN
    row = iota((plane * RING * extra, tokens), 0)
    slot = (MAIN + row % extra).astype(F32)
    for j in range(RING):
        keep = (spread(ranks[j], RING * extra) == slot) & ((row // extra) % RING == j)
        rest_ref[:, j * tokens : (j + 1) * tokens] = jnp.where(keep, 1.0, 0.0).astype(BF16)


def expert_kernel(
    offset, most, ring_ref, low_ref, high_ref, down_ref, saved_ref, weight_ref, *refs
):
    rest = offset is None
    if rest:
        s0, s1, s2, s3, _, grad_ref, slot_ref, column_ref, total_ref = refs
    elif offset == 0:
        grad_ref, slot_ref, column_ref, total_ref = refs
    else:
        _, grad_ref, slot_ref, column_ref, total_ref = refs
    step = pl.program_id(0)
    rows = column_ref.shape[0]
    half = low_ref.shape[-1]
    plane = weight_ref.shape[0] // 8
    lanes = weight_ref.shape[1]
    extra = most - MAIN
    ring = ring_ref[0]

    def decode(i):
        source = i // MAIN
        if rest:
            return source, (i // extra) % RING, MAIN + i % extra
        return source, jnp.full(i.shape, offset, jnp.int32), i % MAIN

    @pl.when(step == 0)
    def _():
        source, j, slot = decode(iota((rows, plane * 8), 0))
        pick = jnp.where(iota((rows, plane * 8), 1) == source * 8 + j, 1.0, 0.0).astype(BF16)
        spread_weight = jnp.dot(pick, weight_ref[...], preferred_element_type=F32)
        _, _, slot = decode(iota((rows, lanes), 0))
        column_ref[...] = jnp.sum(
            jnp.where(iota((rows, lanes), 1) == slot, spread_weight, 0.0), axis=1, keepdims=True
        )
        total_ref[...] = jnp.zeros_like(total_ref)

    dims = (((1,), (1,)), ((), ()))
    low = low_ref[...].reshape(rows, half)
    high = high_ref[...].reshape(rows, half)
    back = lax.dot_general(low, down_ref[:, :half], dims, preferred_element_type=F32)
    back += lax.dot_general(high, down_ref[:, half:], dims, preferred_element_type=F32)

    source, j, slot = decode(iota((rows, rows), 1))
    if rest:
        out_row = (slot - MAIN) * (plane * RING) + ((ring + j) % RING) * plane + source
    else:
        out_row = slot * plane + source
    move = jnp.where(iota((rows, rows), 0) == out_row, 1.0, 0.0).astype(BF16)

    grad = (column_ref[...] * back).astype(BF16)
    moved = jnp.dot(move, grad, preferred_element_type=F32).astype(BF16)
    grad_ref[...] = moved.reshape(grad_ref.shape)
    saved = saved_ref[...].reshape(rows, saved_ref.shape[-1])
    saved = lax.dot_general(move, saved, (((0,), (0,)), ((), ())), preferred_element_type=F32)
    total_ref[...] += jnp.sum(saved * back, axis=1, keepdims=True)

    @pl.when(step == pl.num_programs(0) - 1)
    def _():
        _, _, slot = decode(iota((rows, lanes), 0))
        wide = jnp.where(iota((rows, lanes), 1) == slot, total_ref[...], 0.0)
        count = RING * plane if rest else plane
        source, j, _ = decode(iota((count, rows), 1))
        row = iota((count, rows), 0)
        here = (row == j * plane + source) if rest else (row == source)
        slots = jnp.dot(
            jnp.where(here, 1.0, 0.0), wide, precision=HIGH, preferred_element_type=F32
        )
        if rest:
            for k, ref in enumerate((s0, s1, s2, s3)):
                slot_ref[(ring + k) % RING] = ref[...] + slots[k * plane : (k + 1) * plane, :]
        else:
            slot_ref[...] = slots


def gate_kernel(most, got_ref, rank_ref, meta_ref, out_ref):
    top = out_ref.shape[0]
    got, rank = got_ref[...], rank_ref[...]
    value = jnp.zeros(rank.shape, F32)
    for r in range(most):
        value = jnp.where(rank == float(r), got[:, r : r + 1], value)
    ids = meta_ref[0:top, :].astype(F32)
    experts = iota(rank.shape, 0).astype(F32)
    for k in range(top):
        out_ref[k : k + 1, :] = jnp.sum(
            jnp.where(ids[k : k + 1, :] == experts, value, 0.0), axis=0, keepdims=True
        )


def project(interpret, offset, most, ring, parts, down, saved, weight, before, prior):
    rest = offset is None
    hidden, width = down.shape
    half = width // 2
    slots, blocks, _ = saved.shape
    plane = blocks // RING
    rows = plane * MAIN
    tile = min(256, hidden)
    low, high, low_spec, high_spec = parts
    if rest:
        extra = most - MAIN
        grad_block = pl.BlockSpec((extra, blocks, tile), lambda n, ring: (MAIN // extra, 0, n))
    else:
        grad_block = pl.BlockSpec(
            (MAIN, plane, tile), lambda n, ring: (0, (ring[0] + offset) % RING, n)
        )
    slot_shape = (RING, plane, 128) if rest else (plane, 128)
    whole = lambda shape: pl.BlockSpec(shape, lambda n, ring: (0,) * len(shape))
    operands = [low, high, down, saved, weight]
    in_specs = [
        low_spec,
        high_spec,
        pl.BlockSpec((tile, width), lambda n, ring: (n, 0)),
        grad_block,
        whole(weight.shape),
    ]
    aliases = {}
    for slot in prior:
        operands.append(slot)
        in_specs.append(whole(slot.shape))
    if before is not None:
        aliases = {1 + len(operands): 0}
        operands.append(before)
        in_specs.append(pl.BlockSpec(memory_space=pl.ANY))
    return pl.pallas_call(
        functools.partial(expert_kernel, offset, most),
        grid_spec=pltpu.PrefetchScalarGridSpec(
            num_scalar_prefetch=1,
            grid=(hidden // tile,),
            in_specs=in_specs,
            out_specs=[grad_block, whole(slot_shape)],
            scratch_shapes=[pltpu.VMEM((rows, 1), F32), pltpu.VMEM((rows, 1), F32)],
        ),
        out_shape=[
            jax.ShapeDtypeStruct((slots, blocks, hidden), BF16),
            jax.ShapeDtypeStruct(slot_shape, F32),
        ],
        input_output_aliases=aliases,
        cost_estimate=pl.CostEstimate(
            flops=2 * rows * hidden * width,
            bytes_accessed=2 * hidden * width + 2 * rows * (width + 2 * hidden),
            transcendentals=0,
        ),
        compiler_params=pltpu.CompilerParams(vmem_limit_bytes=32 * 1024 * 1024),
        interpret=interpret,
        name="rest_rows" if rest else f"rows_{offset}",
    )(ring, *operands)


def small_call(kernel, ring, operands, outs, name, interpret):
    specs = [pl.BlockSpec(memory_space=pltpu.VMEM)] * len(operands)
    if ring is not None:
        operands = [ring] + operands
        specs = [pl.BlockSpec(memory_space=pltpu.SMEM)] + specs
    return pl.pallas_call(
        kernel,
        in_specs=specs,
        out_specs=[pl.BlockSpec(memory_space=pltpu.VMEM)] * len(outs),
        out_shape=outs,
        cost_estimate=pl.CostEstimate(flops=10**6, bytes_accessed=10**6, transcendentals=0),
        interpret=interpret,
        name=name,
    )(*operands)


def pick_rows(pick, rows):
    return jnp.dot(pick, rows, preferred_element_type=F32).astype(BF16)


def exchange(rows):
    plane = lax.axis_size("plane")
    split = rows.reshape(plane, -1, rows.shape[1])
    return lax.all_to_all(split, "plane", split_axis=0, concat_axis=0, tiled=True)


def local(interpret, grad_out, expert_ids, gate_weights, down_weight, hidden_saved):
    plane = lax.axis_size("plane")
    sections = lax.axis_size("section")
    blocks, most, hidden = hidden_saved.shape[2:]
    width = grad_out.shape[2]
    half = width // 2
    tokens, top = expert_ids.shape[1:]
    ring = lax.axis_index("ring").astype(jnp.int32).reshape(1)
    move = lambda j, x: lax.ppermute(x, "ring", [((i + j) % RING, i) for i in range(RING)])

    x0 = lax.ppermute(grad_out[0], "section", [(i, (i - 1) % sections) for i in range(sections)])
    meta0 = jnp.concatenate([expert_ids[0].T.astype(BF16), gate_weights[0].T], axis=0)
    metas = [meta0] + [move(j, meta0) for j in (1, 2, 3)]

    rows = plane * MAIN
    S = jax.ShapeDtypeStruct
    rank, pick0 = small_call(
        own_index_kernel, ring, [meta0], [S((blocks, tokens), F32), S((rows, tokens), BF16)],
        "own_index", interpret,
    )
    x0l, x0h = x0[:, :half], x0[:, half:]
    x1l, x3l = move(1, x0l), move(3, x0l)
    x1h, x3h = move(1, x0h), move(3, x0h)
    x2l, x2h = move(1, x1l), move(3, x3h)

    got0 = exchange(pick_rows(pick0, x0))
    pick_side, pick_far, pick_rest, weight = small_call(
        functools.partial(index_kernel, most), ring, metas,
        [
            S((2 * rows, 2 * tokens), BF16),
            S((rows, tokens), BF16),
            S((plane * RING * (most - MAIN), RING * tokens), BF16),
            S((plane * 8, 128), BF16),
        ],
        "index", interpret,
    )
    weight = exchange(weight).reshape(plane * 8, 128)
    got_l = exchange(pick_rows(pick_side, jnp.concatenate([x1l, x3l], axis=0)))
    got_h = exchange(pick_rows(pick_side, jnp.concatenate([x1h, x3h], axis=0)))
    x2 = jnp.concatenate([x2l, x2h], axis=1)
    got2 = exchange(pick_rows(pick_far, x2))
    x_all = jnp.concatenate(
        [x0, jnp.concatenate([x1l, x1h], 1), x2, jnp.concatenate([x3l, x3h], 1)], axis=0
    )
    got_rest = exchange(pick_rows(pick_rest, x_all))

    down = down_weight[0, 0]
    saved = hidden_saved[0, 0].transpose(1, 0, 2)
    part_specs = [pl.BlockSpec((rows, half), lambda n, ring, c=c: (0, c)) for c in range(2)]

    def both(got):
        flat = got.reshape(rows, width)
        return (flat, flat, *part_specs)

    def side(s):
        spec = pl.BlockSpec((plane, None, MAIN, half), lambda n, ring: (0, s, 0, 0))
        shape = (plane, 2, MAIN, half)
        return (got_l.reshape(shape), got_h.reshape(shape), spec, spec)

    run = functools.partial(project, interpret)
    grad, s0 = run(0, most, ring, both(got0), down, saved, weight, None, [])
    grad, s1 = run(1, most, ring, side(0), down, saved, weight, grad, [])
    grad, s3 = run(3, most, ring, side(1), down, saved, weight, grad, [])
    grad, s2 = run(2, most, ring, both(got2), down, saved, weight, grad, [])
    grad, slots = run(None, most, ring, both(got_rest), down, saved, weight, grad, [s0, s1, s2, s3])

    returned = lax.all_to_all(
        slots.reshape(blocks, 1, 128), ("ring", "plane"), split_axis=0, concat_axis=0, tiled=True
    )
    gate = small_call(
        functools.partial(gate_kernel, most), None, [returned.reshape(blocks, 128), rank, meta0],
        [S((top, tokens), F32)], "gate", interpret,
    )[0]
    return (grad.transpose(1, 0, 2)[None, None], gate.T[None])


def solution(mesh, interpret=False):
    sections, experts = mesh.devices.shape
    fine = Mesh(mesh.devices.reshape(sections, RING, experts // RING), ("section", "ring", "plane"))
    both = ("ring", "plane")
    in_specs = (
        P("section", both, None),
        P("section", both, None),
        P("section", both, None),
        P("section", both, None, None),
        P("section", both, None, None, None),
    )
    out_specs = (P("section", both, None, None, None), P("section", both, None))
    return jax.shard_map(
        functools.partial(local, interpret), mesh=fine, in_specs=in_specs, out_specs=out_specs, check_vma=False
    )
```

time: 439 us -> 230 us (0.52)
  waiting for transfers between devices: 235 us -> 65.6 us
  local copies, waits for them, and re-layouts: 110 us -> 15.8 us
  Pallas kernels: 0 us -> 39.2 us
  blocking collectives: 0 us -> 20.8 us
  other arithmetic: 19.8 us -> 1.37 us
  starting transfers between devices: 49.5 us -> 62.3 us
    all_to_all x3 -> x6, waiting for transfers between devices: 235 us -> 13 us  [exchange(): lax.all_to_all(split, 'plane', split_axis=0, concat_axis=0, tiled=True)]
    scatter x2 -> x0, local copies, waits for them, and re-layouts: 54.4 us -> none  [the longest x1 46.8 us: pack_rows(): rows = jnp.zeros((experts * most, grad_local.shape[1]), jnp.bfloat16).at[...]
    ppermute x1 -> x10, waiting for transfers between devices: 0.01 us -> 52.6 us  [the longest x9 52.6 us: local(): lax.ppermute(x, 'ring', [((i + j) % RING, i) for i in range(RING)])]
    pallas_call x0 -> x8, Pallas kernels: none -> 39.2 us  [the longest x5 33.8 us: project(): pl.pallas_call(functools.partial(expert_kernel, offset, most), grid_spec=...]
    reshape x5 -> x0, local copies, waits for them, and re-layouts: 30.1 us -> none  [the longest x1 13.2 us: project_back(): flat_rows = rows_in.reshape(-1, rows_in.shape[2])]
    all_to_all x0 -> x1, blocking collectives: none -> 20.8 us  [local(): lax.all_to_all(slots.reshape(blocks, 1, 128), ('ring', 'plane'), split_ax...]
    ppermute x1 -> x10, starting transfers between devices: 1.43 us -> 21.4 us  [the longest x9 20 us: local(): lax.ppermute(x, 'ring', [((i + j) % RING, i) for i in range(RING)])]
    another operation x3 -> x0, other arithmetic: 18.2 us -> none
  transfers between devices with their start and end apart: 4 -> 16, of which waited for: 2 -> 9; matrix products, arithmetic and copies ran while one was open for 25% -> 10% of each run, Pallas kernels for 0% -> 13%
where the time goes in v1:
time: 230 us; the launch traced here: 226 us
  waiting for transfers between devices  65.6 us (29%)
  starting transfers between devices  62.3 us (27%)
  Pallas kernels  39.2 us (17%)
  blocking collectives  20.8 us (9%)
  matrix products  20.1 us (9%)
  local copies, waits for them, and re-layouts  15.8 us (7%)
    ppermute x9, waiting for transfers between devices, local(): lax.ppermute(x, 'ring', [((i + j) % RING, i) for i in range(RING)])  52.6 us
    all_to_all x6, starting transfers between devices, exchange(): lax.all_to_all(split, 'plane', split_axis=0, concat_axis=0, tiled=True)  40.9 us
    pallas_call x5, Pallas kernels, project(): pl.pallas_call(functools.partial(expert_kernel, offset, most), grid_spec=...  33.8 us
    all_to_all x1, blocking collectives, local(): lax.all_to_all(slots.reshape(blocks, 1, 128), ('ring', 'plane'), split_ax...  20.8 us
    dot_general x5, matrix products, pick_rows(): return jnp.dot(pick, rows, preferred_element_type=F32).astype(BF16)  20.1 us
    ppermute x9, starting transfers between devices, local(): lax.ppermute(x, 'ring', [((i + j) % RING, i) for i in range(RING)])  20 us
    unnamed x49, local copies, waits for them, and re-layouts  15.8 us
    all_to_all x6, waiting for transfers between devices, exchange(): lax.all_to_all(split, 'plane', split_axis=0, concat_axis=0, tiled=True)  13 us
  transfers between devices with their start and end apart: 16, of which 9 were waited for; matrix products, arithmetic and copies ran while one was open for 10% of the time, Pallas kernels for 13%

profile of v1, /device:TPU:2, one launch (start us, length us, event | category | flops | bytes accessed | tf_op | source)
XLA Modules:
  0.0 226.1 jit_solution(18151767020597027476)
XLA Ops:
  0.6 1.4 collective-permute-start.3
  2.1 0.7 convert_bitcast_fusion
  3.4 5.4 %collective-permute-start = (bf16[16,128]{1,0:T(8,128)(2,1)S(1)}, bf16[16,128]{1,0:T(8,128)(2,1)S(1)}, u32[]{:S(2)}, u32[]{:S(2)}) collective-permute-start(bf16[16,128]{1,0:T(8,128)(2,1)S(1)} %pad_maximum_fusion.m0_ref.meta_ref), channel_id=1, source_target_pairs={{16,0},{32,16},{48,32},{0,48},{17,1},{33,17},{49,33},{1,49},{18,2}... | collective-permute-start | bytes 12296 | tf_op jit(solution)/shard_map/ppermute | solution.py:275
  8.8 1.4 collective-permute-start.1
  10.3 2.4 %collective-permute-start.2 = (bf16[16,128]{1,0:T(8,128)(2,1)S(1)}, bf16[16,128]{1,0:T(8,128)(2,1)S(1)}, u32[]{:S(2)}, u32[]{:S(2)}) collective-permute-start(bf16[16,128]{1,0:T(8,128)(2,1)S(1)} %pad_maximum_fusion.m0_ref.meta_ref), channel_id=1, source_target_pairs={{48,0},{0,16},{16,32},{32,48},{49,1},{1,17},{17,33},{33,49},{50,2}... | collective-permute-start | bytes 12296 | tf_op jit(solution)/shard_map/ppermute | solution.py:275
  12.7 1.6 own_index.1
  14.3 5.9 %collective-permute-done.1.m2_ref = bf16[16,128]{1,0:T(8,128)(2,1)S(1)} collective-permute-done((bf16[16,128]{1,0:T(8,128)(2,1)S(1)}, bf16[16,128]{1,0:T(8,128)(2,1)S(1)}, u32[]{:S(2)}, u32[]{:S(2)}) %collective-permute-start.1) | collective-permute-done | bytes 4128 | tf_op jit(solution)/shard_map/ppermute | solution.py:275
  21.4 2.2 index.1
  23.5 7.5 %all-to-all-start.1 = ((bf16[16,8,128]{2,1,0:T(8,128)(2,1)}), bf16[16,8,128]{2,1,0:T(8,128)(2,1)S(1)}, u32[]{:S(2)}, u32[]{:S(2)}) async-start(bf16[16,8,128]{2,1,0:T(8,128)(2,1)} %bitcast.68), calls=%async_computation.1 | async-start | bytes 65536 | tf_op jit(solution)/shard_map/all_to_all | solution.py:264
  31.0 2.7 %convolution_convert_fusion.1 = bf16[256,3584]{1,0:T(8,128)(2,1)} fusion(bf16[256,128]{1,0:T(8,128)(2,1)} %get-tuple-element.20, bf16[128,3584]{1,0:T(8,128)(2,1)S(1)} %collective-permute-done.3), kind=kOutput, calls=%fused_computation.1 | convolution fusion | flops 235798528 | bytes 2818048 | tf_op jit(solution)/shard_map/dot_general | solution.py:258
  33.7 3.4 %all-to-all-done.1 = bf16[16,8,128]{2,1,0:T(8,128)(2,1)S(1)} async-done(((bf16[16,8,128]{2,1,0:T(8,128)(2,1)}), bf16[16,8,128]{2,1,0:T(8,128)(2,1)S(1)}, u32[]{:S(2)}, u32[]{:S(2)}) %all-to-all-start.1) | async-done | bytes 32800 | tf_op jit(solution)/shard_map/all_to_all | solution.py:264
  37.1 5.2 %all-to-all-start.2 = ((bf16[16,16,3584]{2,1,0:T(8,128)(2,1)}), bf16[16,16,3584]{2,1,0:T(8,128)(2,1)S(1)}, u32[]{:S(2)}, u32[]{:S(2)}) async-start(bf16[16,16,3584]{2,1,0:T(8,128)(2,1)} %bitcast.64), calls=%async_computation.2 | async-start | bytes 3670016 | tf_op jit(solution)/shard_map/all_to_all | solution.py:264
  42.4 0.7 collective-permute-start.4
  43.1 2.3 %collective-permute-start.9 = (bf16[128,1792]{1,0:T(8,128)(2,1)S(1)}, bf16[128,1792]{1,0:T(8,128)(2,1)S(1)}, u32[]{:S(2)}, u32[]{:S(2)}) collective-permute-start(bf16[128,1792]{1,0:T(8,128)(2,1)S(1)} %get-tuple-element.34), channel_id=1, source_target_pairs={{48,0},{0,16},{16,32},{32,48},{49,1},{1,17},{17,33},{33,49},{50,2}... | collective-permute-start | bytes 1376264 | tf_op jit(solution)/shard_map/ppermute | solution.py:275
  45.4 13.3 %collective-permute-done.4 = bf16[128,1792]{1,0:T(8,128)(2,1)S(1)} collective-permute-done((bf16[128,1792]{1,0:T(8,128)(2,1)S(1)}, bf16[128,1792]{1,0:T(8,128)(2,1)S(1)}, u32[]{:S(2)}, u32[]{:S(2)}) %collective-permute-start.4) | collective-permute-done | bytes 458784 | tf_op jit(solution)/shard_map/ppermute | solution.py:275
  58.8 1.4 collective-permute-done.9
  60.2 0.8 copy-done.13
  61.0 1.9 convolution_convert_fusion.4
  62.9 1.2 copy-done.6
  64.2 7.3 %all-to-all-start.3 = ((bf16[16,32,1792]{2,1,0:T(8,128)(2,1)}), bf16[16,32,1792]{2,1,0:T(8,128)(2,1)S(1)}, u32[]{:S(2)}, u32[]{:S(2)}) async-start(bf16[16,32,1792]{2,1,0:T(8,128)(2,1)} %bitcast.65), calls=%async_computation.3 | async-start | bytes 3670016 | tf_op jit(solution)/shard_map/all_to_all | solution.py:264
  71.5 1.0 collective-permute-start.7
  72.5 3.1 %collective-permute-start.5 = (bf16[128,1792]{1,0:T(8,128)(2,1)S(1)}, bf16[128,1792]{1,0:T(8,128)(2,1)S(1)}, u32[]{:S(2)}, u32[]{:S(2)}) collective-permute-start(bf16[128,1792]{1,0:T(8,128)(2,1)S(1)} %get-tuple-element.35), channel_id=1, source_target_pairs={{16,0},{32,16},{48,32},{0,48},{17,1},{33,17},{49,33},{1,49},{18,2}... | collective-permute-start | bytes 1376264 | tf_op jit(solution)/shard_map/ppermute | solution.py:275
  75.6 10.9 %collective-permute-done.7 = bf16[128,1792]{1,0:T(8,128)(2,1)S(1)} collective-permute-done((bf16[128,1792]{1,0:T(8,128)(2,1)S(1)}, bf16[128,1792]{1,0:T(8,128)(2,1)S(1)}, u32[]{:S(2)}, u32[]{:S(2)}) %collective-permute-start.7) | collective-permute-done | bytes 458784 | tf_op jit(solution)/shard_map/ppermute | solution.py:275
  86.5 5.4 %collective-permute-done.5 = bf16[128,1792]{1,0:T(8,128)(2,1)S(1)} collective-permute-done((bf16[128,1792]{1,0:T(8,128)(2,1)S(1)}, bf16[128,1792]{1,0:T(8,128)(2,1)S(1)}, u32[]{:S(2)}, u32[]{:S(2)}) %collective-permute-start.5) | collective-permute-done | bytes 458784 | tf_op jit(solution)/shard_map/ppermute | solution.py:275
  91.9 0.8 copy-done.17
  92.7 1.9 convolution_convert_fusion.3
  94.6 7.4 %all-to-all-start.4 = ((bf16[16,32,1792]{2,1,0:T(8,128)(2,1)}), bf16[16,32,1792]{2,1,0:T(8,128)(2,1)}, u32[]{:S(2)}, u32[]{:S(2)}) async-start(bf16[16,32,1792]{2,1,0:T(8,128)(2,1)} %bitcast.63), calls=%async_computation.4 | async-start | bytes 3670016 | tf_op jit(solution)/shard_map/all_to_all | solution.py:264
  101.9 1.0 collective-permute-start.6
  102.9 2.6 %collective-permute-start.8 = (bf16[128,1792]{1,0:T(8,128)(2,1)S(1)}, bf16[128,1792]{1,0:T(8,128)(2,1)S(1)}, u32[]{:S(2)}, u32[]{:S(2)}) collective-permute-start(bf16[128,1792]{1,0:T(8,128)(2,1)S(1)} %copy-done.16), channel_id=1, source_target_pairs={{48,0},{0,16},{16,32},{32,48},{49,1},{1,17},{17,33},{33,49},{50,2}... | collective-permute-start | bytes 1376264 | tf_op jit(solution)/shard_map/ppermute | solution.py:275
  105.6 14.6 %collective-permute-done.6 = bf16[128,1792]{1,0:T(8,128)(2,1)S(1)} collective-permute-done((bf16[128,1792]{1,0:T(8,128)(2,1)}, bf16[128,1792]{1,0:T(8,128)(2,1)S(1)}, u32[]{:S(2)}, u32[]{:S(2)}) %collective-permute-start.6) | collective-permute-done | bytes 458784 | tf_op jit(solution)/shard_map/ppermute | solution.py:275
  120.2 1.0 collective-permute-done.8
  121.2 1.0 copy-done.8
  122.2 1.9 convolution_convert_fusion
  124.1 7.4 %all-to-all-start.5 = ((bf16[16,16,3584]{2,1,0:T(8,128)(2,1)}), bf16[16,16,3584]{2,1,0:T(8,128)(2,1)}, u32[]{:S(2)}, u32[]{:S(2)}) async-start(bf16[16,16,3584]{2,1,0:T(8,128)(2,1)} %bitcast.20), calls=%async_computation.5 | async-start | bytes 3670016 | tf_op jit(solution)/shard_map/all_to_all | solution.py:264
  131.5 11.8 %convolution_convert_fusion.2 = bf16[256,3584]{1,0:T(8,128)(2,1)} fusion(bf16[256,512]{1,0:T(8,128)(2,1)S(1)} %copy-done.23, bf16[128,1792]{1,0:T(8,128)(2,1)S(1)} %copy-done.16, bf16[128,1792]{1,0:T(8,128)(2,1)S(1)} %copy-done.14, bf16[128,3584]{1,0:T(8,128)(2,1)S(1)} %copy-done.9, bf16[128,1792]{1,0:T(8,128)(2,1)} %copy-done.17, ...), kind=kOutput, calls=%fused_computation.2 | convolution fusion | flops 962461696 | bytes 5767168 | tf_op jit(solution)/shard_map/dot_general | solution.py:258
  143.2 9.6 %all-to-all-done.5 = bf16[16,16,3584]{2,1,0:T(8,128)(2,1)} async-done(((bf16[16,16,3584]{2,1,0:T(8,128)(2,1)}), bf16[16,16,3584]{2,1,0:T(8,128)(2,1)}, u32[]{:S(2)}, u32[]{:S(2)}) %all-to-all-start.5) | async-done | bytes 1835040 | tf_op jit(solution)/shard_map/all_to_all | solution.py:264
  152.8 6.2 %all-to-all-start = ((bf16[16,16,3584]{2,1,0:T(8,128)(2,1)}), bf16[16,16,3584]{2,1,0:T(8,128)(2,1)}, u32[]{:S(2)}, u32[]{:S(2)}) async-start(bf16[16,16,3584]{2,1,0:T(8,128)(2,1)} %bitcast.66), calls=%async_computation | async-start | bytes 3670016 | tf_op jit(solution)/shard_map/all_to_all | solution.py:264
  159.0 3.1 %copy-done = bf16[1,1,1024,3584]{3,2,1,0:T(8,128)(2,1)S(1)} copy-done((bf16[1,1,1024,3584]{3,2,1,0:T(8,128)(2,1)S(1)}, bf16[1,1,1024,3584]{3,2,1,0:T(8,128)(2,1)}, u32[]{:S(2)}) %copy-start) | copy-done | bytes 7340056
  162.1 1.5 copy-done.7
  163.6 5.8 %rows_0.1 = (bf16[20,64,1024]{2,1,0:T(8,128)(2,1)}, f32[16,128]{1,0:T(8,128)S(1)}) custom-call(s32[1]{0:T(128)} %bitcast.ring_ref, bf16[256,3584]{1,0:T(8,128)(2,1)S(1)} %bitcast.54, bf16[256,3584]{1,0:T(8,128)(2,1)S(1)} %bitcast.55, bf16[1024,3584]{1,0:T(8,128)(2,1)S(1)} %bitcast.42, bf16[20,64,1024]{2,1,0:T(8,128)(2,1)S(1)} %bitcast.47, ...), custom_call_target="tpu_custom_call" | custom-call | flops 1879048192 | bytes 10223616 | tf_op jit(solution)/shard_map/rows_0/pallas_call | solution.py:216
  169.4 3.1 %copy-done.1 = bf16[1,1,1024,3584]{3,2,1,0:T(8,128)(2,1)S(1)} copy-done((bf16[1,1,1024,3584]{3,2,1,0:T(8,128)(2,1)S(1)}, bf16[1,1,1024,3584]{3,2,1,0:T(8,128)(2,1)}, u32[]{:S(2)}) %copy-start.1) | copy-done | bytes 7340056
  172.5 6.9 %rows_1.1 = (bf16[20,64,1024]{2,1,0:T(8,128)(2,1)}, f32[16,128]{1,0:T(8,128)S(1)}) custom-call(s32[1]{0:T(128)} %bitcast.ring_ref, bf16[16,2,16,1792]{3,2,1,0:T(8,128)(2,1)S(1)} %bitcast.52, bf16[16,2,16,1792]{3,2,1,0:T(8,128)(2,1)} %bitcast.19.high_ref, bf16[1024,3584]{1,0:T(8,128)(2,1)S(1)} %bitcast.43, ...), custom_call_target="tpu_custom_call", output_to_operand_aliasing={{0}: (6, {})} | custom-call | flops 1879048192 | bytes 10223616 | tf_op jit(solution)/shard_map/rows_1/pallas_call | solution.py:216
  179.4 6.9 %rows_3.1 = (bf16[20,64,1024]{2,1,0:T(8,128)(2,1)}, f32[16,128]{1,0:T(8,128)S(1)}) custom-call(s32[1]{0:T(128)} %bitcast.ring_ref, bf16[16,2,16,1792]{3,2,1,0:T(8,128)(2,1)S(1)} %bitcast.53, bf16[16,2,16,1792]{3,2,1,0:T(8,128)(2,1)} %bitcast.19.high_ref, bf16[1024,3584]{1,0:T(8,128)(2,1)S(1)} %bitcast.44, ...), custom_call_target="tpu_custom_call", output_to_operand_aliasing={{0}: (6, {})} | custom-call | flops 1879048192 | bytes 10223616 | tf_op jit(solution)/shard_map/rows_3/pallas_call | solution.py:216
  186.3 7.1 %rows_2.1 = (bf16[20,64,1024]{2,1,0:T(8,128)(2,1)}, f32[16,128]{1,0:T(8,128)S(1)}) custom-call(s32[1]{0:T(128)} %bitcast.ring_ref, bf16[256,3584]{1,0:T(8,128)(2,1)} %bitcast.21.low_ref.high_ref, bf16[256,3584]{1,0:T(8,128)(2,1)} %bitcast.21.low_ref.high_ref, bf16[1024,3584]{1,0:T(8,128)(2,1)S(1)} %bitcast.45, ...), custom_call_target="tpu_custom_call", output_to_operand_aliasing={{0}: (6, {})} | custom-call | flops 1879048192 | bytes 10223616 | tf_op jit(solution)/shard_map/rows_2/pallas_call | solution.py:216
  193.4 3.1 %copy-done.2 = bf16[1,1,1024,3584]{3,2,1,0:T(8,128)(2,1)S(1)} copy-done((bf16[1,1,1024,3584]{3,2,1,0:T(8,128)(2,1)S(1)}, bf16[1,1,1024,3584]{3,2,1,0:T(8,128)(2,1)}, u32[]{:S(2)}) %copy-start.2) | copy-done | bytes 7340056
  196.5 7.1 %rest_rows.1 = (bf16[20,64,1024]{2,1,0:T(8,128)(2,1)}, f32[4,16,128]{2,1,0:T(8,128)S(1)}) custom-call(s32[1]{0:T(128)} %bitcast.ring_ref, bf16[256,3584]{1,0:T(8,128)(2,1)} %bitcast.7.low_ref.high_ref, bf16[256,3584]{1,0:T(8,128)(2,1)} %bitcast.7.low_ref.high_ref, bf16[1024,3584]{1,0:T(8,128)(2,1)S(1)} %bitcast.46, ...), custom_call_target="tpu_custom_call", output_to_operand_aliasing={{0}: (10, {})} | custom-call | flops 1879048192 | bytes 10223616 | tf_op jit(solution)/shard_map/rest_rows/pallas_call | solution.py:216
  203.6 20.8 %all_to_all.35 = f32[64,1,128]{2,1,0:T(1,128)} all-to-all(f32[64,1,128]{2,1,0:T(1,128)S(1)} %bitcast.61), channel_id=1, replica_groups=mesh['section'=4,'ring'=4,'plane'=16] {'ring','plane'}, dimensions={0} | all-to-all | bytes 65536 | tf_op jit(solution)/shard_map/all_to_all | solution.py:333
  224.4 1.7 gate.1
  (51 shorter events, 2.1 us)
Async XLA Ops:
  0.6 30.4 %collective-permute-start.3 = (bf16[128,3584]{1,0:T(8,128)(2,1)}, bf16[128,3584]{1,0:T(8,128)(2,1)S(1)}, u32[]{:S(2)}, u32[]{:S(2)}) collective-permute-start(bf16[128,3584]{1,0:T(8,128)(2,1)} %bitcast.71), channel_id=1, source_target_pairs={{0,192},{64,0},{128,64},{192,128},{1,193},{65,1},{129,65},{193,129... | collective-permute-start | bytes 2752520 | tf_op jit(solution)/shard_map/ppermute | solution.py:277
  3.4 9.2 %copy-start.19 = (bf16[16,128]{1,0:T(8,128)(2,1)}, bf16[16,128]{1,0:T(8,128)(2,1)S(1)}, u32[]{:S(2)}) copy-start(bf16[16,128]{1,0:T(8,128)(2,1)S(1)} %pad_maximum_fusion.m0_ref.meta_ref) | copy-start | bytes 12292
  3.4 10.8 %collective-permute-start = (bf16[16,128]{1,0:T(8,128)(2,1)S(1)}, bf16[16,128]{1,0:T(8,128)(2,1)S(1)}, u32[]{:S(2)}, u32[]{:S(2)}) collective-permute-start(bf16[16,128]{1,0:T(8,128)(2,1)S(1)} %pad_maximum_fusion.m0_ref.meta_ref), channel_id=1, source_target_pairs={{16,0},{32,16},{48,32},{0,48},{17,1},{33,17},{49,33},{1,49},{18,2}... | collective-permute-start | bytes 12296 | tf_op jit(solution)/shard_map/ppermute | solution.py:275
  8.8 11.4 %collective-permute-start.1 = (bf16[16,128]{1,0:T(8,128)(2,1)S(1)}, bf16[16,128]{1,0:T(8,128)(2,1)S(1)}, u32[]{:S(2)}, u32[]{:S(2)}) collective-permute-start(bf16[16,128]{1,0:T(8,128)(2,1)S(1)} %pad_maximum_fusion.m0_ref.meta_ref), channel_id=1, source_target_pairs={{32,0},{48,16},{0,32},{16,48},{33,1},{49,17},{1,33},{17,49},{34,2}... | collective-permute-start | bytes 12296 | tf_op jit(solution)/shard_map/ppermute | solution.py:275
  10.3 9.9 %collective-permute-start.2 = (bf16[16,128]{1,0:T(8,128)(2,1)S(1)}, bf16[16,128]{1,0:T(8,128)(2,1)S(1)}, u32[]{:S(2)}, u32[]{:S(2)}) collective-permute-start(bf16[16,128]{1,0:T(8,128)(2,1)S(1)} %pad_maximum_fusion.m0_ref.meta_ref), channel_id=1, source_target_pairs={{48,0},{0,16},{16,32},{32,48},{49,1},{1,17},{17,33},{33,49},{50,2}... | collective-permute-start | bytes 12296 | tf_op jit(solution)/shard_map/ppermute | solution.py:275
  14.3 6.0 %copy-start.20 = (bf16[16,128]{1,0:T(8,128)(2,1)}, bf16[16,128]{1,0:T(8,128)(2,1)S(1)}, u32[]{:S(2)}) copy-start(bf16[16,128]{1,0:T(8,128)(2,1)S(1)} %collective-permute-done.m1_ref) | copy-start | bytes 12292
  20.2 0.6 copy-start.21
  20.8 0.6 copy-start.22
  23.5 13.6 %all-to-all-start.1 = ((bf16[16,8,128]{2,1,0:T(8,128)(2,1)}), bf16[16,8,128]{2,1,0:T(8,128)(2,1)S(1)}, u32[]{:S(2)}, u32[]{:S(2)}) async-start(bf16[16,8,128]{2,1,0:T(8,128)(2,1)} %bitcast.68), calls=%async_computation.1 | async-start | bytes 65536 | tf_op jit(solution)/shard_map/all_to_all | solution.py:264
  37.1 23.9 %copy-start.10 = (bf16[512,256]{1,0:T(8,128)(2,1)S(1)}, bf16[512,256]{1,0:T(8,128)(2,1)}, u32[]{:S(2)}) copy-start(bf16[512,256]{1,0:T(8,128)(2,1)} %get-tuple-element.22) | copy-start | bytes 786436
  37.1 25.8 %all-to-all-start.2 = ((bf16[16,16,3584]{2,1,0:T(8,128)(2,1)}), bf16[16,16,3584]{2,1,0:T(8,128)(2,1)S(1)}, u32[]{:S(2)}, u32[]{:S(2)}) async-start(bf16[16,16,3584]{2,1,0:T(8,128)(2,1)} %bitcast.64), calls=%async_computation.2 | async-start | bytes 3670016 | tf_op jit(solution)/shard_map/all_to_all | solution.py:264
  42.4 16.3 %collective-permute-start.4 = (bf16[128,1792]{1,0:T(8,128)(2,1)S(1)}, bf16[128,1792]{1,0:T(8,128)(2,1)S(1)}, u32[]{:S(2)}, u32[]{:S(2)}) collective-permute-start(bf16[128,1792]{1,0:T(8,128)(2,1)S(1)} %get-tuple-element.34), channel_id=1, source_target_pairs={{16,0},{32,16},{48,32},{0,48},{17,1},{33,17},{49,33},{1,49},{18,2}... | collective-permute-start | bytes 1376264 | tf_op jit(solution)/shard_map/ppermute | solution.py:275
  43.1 17.1 %collective-permute-start.9 = (bf16[128,1792]{1,0:T(8,128)(2,1)S(1)}, bf16[128,1792]{1,0:T(8,128)(2,1)S(1)}, u32[]{:S(2)}, u32[]{:S(2)}) collective-permute-start(bf16[128,1792]{1,0:T(8,128)(2,1)S(1)} %get-tuple-element.34), channel_id=1, source_target_pairs={{48,0},{0,16},{16,32},{32,48},{49,1},{1,17},{17,33},{33,49},{50,2}... | collective-permute-start | bytes 1376264 | tf_op jit(solution)/shard_map/ppermute | solution.py:275
  58.8 1.5 copy-start.11
  60.2 0.8 copy-start.13
  62.9 1.2 copy-start.6
  64.2 30.4 %all-to-all-start.3 = ((bf16[16,32,1792]{2,1,0:T(8,128)(2,1)}), bf16[16,32,1792]{2,1,0:T(8,128)(2,1)S(1)}, u32[]{:S(2)}, u32[]{:S(2)}) async-start(bf16[16,32,1792]{2,1,0:T(8,128)(2,1)} %bitcast.65), calls=%async_computation.3 | async-start | bytes 3670016 | tf_op jit(solution)/shard_map/all_to_all | solution.py:264
  71.5 15.1 %collective-permute-start.7 = (bf16[128,1792]{1,0:T(8,128)(2,1)S(1)}, bf16[128,1792]{1,0:T(8,128)(2,1)S(1)}, u32[]{:S(2)}, u32[]{:S(2)}) collective-permute-start(bf16[128,1792]{1,0:T(8,128)(2,1)S(1)} %get-tuple-element.35), channel_id=1, source_target_pairs={{48,0},{0,16},{16,32},{32,48},{49,1},{1,17},{17,33},{33,49},{50,2}... | collective-permute-start | bytes 1376264 | tf_op jit(solution)/shard_map/ppermute | solution.py:275
  72.5 19.4 %collective-permute-start.5 = (bf16[128,1792]{1,0:T(8,128)(2,1)S(1)}, bf16[128,1792]{1,0:T(8,128)(2,1)S(1)}, u32[]{:S(2)}, u32[]{:S(2)}) collective-permute-start(bf16[128,1792]{1,0:T(8,128)(2,1)S(1)} %get-tuple-element.35), channel_id=1, source_target_pairs={{16,0},{32,16},{48,32},{0,48},{17,1},{33,17},{49,33},{1,49},{18,2}... | collective-permute-start | bytes 1376264 | tf_op jit(solution)/shard_map/ppermute | solution.py:275
  86.5 5.4 %copy-start.15 = (bf16[128,1792]{1,0:T(8,128)(2,1)}, bf16[128,1792]{1,0:T(8,128)(2,1)S(1)}, u32[]{:S(2)}) copy-start(bf16[128,1792]{1,0:T(8,128)(2,1)S(1)} %collective-permute-done.7) | copy-start | bytes 1376260
  91.9 0.8 copy-start.17
  94.6 8.4 %copy-start.16 = (bf16[128,1792]{1,0:T(8,128)(2,1)S(1)}, bf16[128,1792]{1,0:T(8,128)(2,1)}, u32[]{:S(2)}) copy-start(bf16[128,1792]{1,0:T(8,128)(2,1)} %copy-done.15) | copy-start | bytes 1376260
  94.6 26.6 %copy-start.4 = (bf16[16,32,1792]{2,1,0:T(8,128)(2,1)}, bf16[16,32,1792]{2,1,0:T(8,128)(2,1)S(1)}, u32[]{:S(2)}) copy-start(bf16[16,32,1792]{2,1,0:T(8,128)(2,1)S(1)} %all-to-all-done.3) | copy-start | bytes 5505028
  94.6 27.6 %copy-start.18 = (bf16[256,128]{1,0:T(8,128)(2,1)S(1)}, bf16[256,128]{1,0:T(8,128)(2,1)}, u32[]{:S(2)}) copy-start(bf16[256,128]{1,0:T(8,128)(2,1)} %get-tuple-element.25) | copy-start | bytes 196612
  94.6 29.5 %all-to-all-start.4 = ((bf16[16,32,1792]{2,1,0:T(8,128)(2,1)}), bf16[16,32,1792]{2,1,0:T(8,128)(2,1)}, u32[]{:S(2)}, u32[]{:S(2)}) async-start(bf16[16,32,1792]{2,1,0:T(8,128)(2,1)} %bitcast.63), calls=%async_computation.4 | async-start | bytes 3670016 | tf_op jit(solution)/shard_map/all_to_all | solution.py:264
  101.9 18.2 %collective-permute-start.6 = (bf16[128,1792]{1,0:T(8,128)(2,1)}, bf16[128,1792]{1,0:T(8,128)(2,1)S(1)}, u32[]{:S(2)}, u32[]{:S(2)}) collective-permute-start(bf16[128,1792]{1,0:T(8,128)(2,1)} %copy-done.11), channel_id=1, source_target_pairs={{16,0},{32,16},{48,32},{0,48},{17,1},{33,17},{49,33},{1,49},{18,2}... | collective-permute-start | bytes 1376264 | tf_op jit(solution)/shard_map/ppermute | solution.py:275
  102.9 18.2 %collective-permute-start.8 = (bf16[128,1792]{1,0:T(8,128)(2,1)S(1)}, bf16[128,1792]{1,0:T(8,128)(2,1)S(1)}, u32[]{:S(2)}, u32[]{:S(2)}) collective-permute-start(bf16[128,1792]{1,0:T(8,128)(2,1)S(1)} %copy-done.16), channel_id=1, source_target_pairs={{48,0},{0,16},{16,32},{32,48},{49,1},{1,17},{17,33},{33,49},{50,2}... | collective-permute-start | bytes 1376264 | tf_op jit(solution)/shard_map/ppermute | solution.py:275
  121.2 1.0 copy-start.8
  122.2 9.2 %copy-start.12 = (bf16[128,1792]{1,0:T(8,128)(2,1)S(1)}, bf16[128,1792]{1,0:T(8,128)(2,1)}, u32[]{:S(2)}) copy-start(bf16[128,1792]{1,0:T(8,128)(2,1)} %copy-done.11) | copy-start | bytes 1376260
  122.2 9.2 %copy-start.14 = (bf16[128,1792]{1,0:T(8,128)(2,1)S(1)}, bf16[128,1792]{1,0:T(8,128)(2,1)}, u32[]{:S(2)}) copy-start(bf16[128,1792]{1,0:T(8,128)(2,1)} %copy-done.13) | copy-start | bytes 1376260
  124.1 7.4 %copy-start.9 = (bf16[128,3584]{1,0:T(8,128)(2,1)S(1)}, bf16[128,3584]{1,0:T(8,128)(2,1)}, u32[]{:S(2)}) copy-start(bf16[128,3584]{1,0:T(8,128)(2,1)} %copy-done.8) | copy-start | bytes 2752516
  124.1 7.4 %copy-start.23 = (bf16[256,512]{1,0:T(8,128)(2,1)S(1)}, bf16[256,512]{1,0:T(8,128)(2,1)}, u32[]{:S(2)}) copy-start(bf16[256,512]{1,0:T(8,128)(2,1)} %get-tuple-element.18) | copy-start | bytes 786436
  124.1 28.7 %all-to-all-start.5 = ((bf16[16,16,3584]{2,1,0:T(8,128)(2,1)}), bf16[16,16,3584]{2,1,0:T(8,128)(2,1)}, u32[]{:S(2)}, u32[]{:S(2)}) async-start(bf16[16,16,3584]{2,1,0:T(8,128)(2,1)} %bitcast.20), calls=%async_computation.5 | async-start | bytes 3670016 | tf_op jit(solution)/shard_map/all_to_all | solution.py:264
  143.2 15.8 %copy-start.3 = (bf16[1,1,64,20,1024]{4,2,3,1,0:T(8,128)(2,1)S(1)}, bf16[1,1,64,20,1024]{4,2,3,1,0:T(8,128)(2,1)}, u32[]{:S(2)}) copy-start(bf16[1,1,64,20,1024]{4,2,3,1,0:T(8,128)(2,1)} %param.9) | copy-start | bytes 7864324
  152.8 40.6 %all-to-all-start = ((bf16[16,16,3584]{2,1,0:T(8,128)(2,1)}), bf16[16,16,3584]{2,1,0:T(8,128)(2,1)}, u32[]{:S(2)}, u32[]{:S(2)}) async-start(bf16[16,16,3584]{2,1,0:T(8,128)(2,1)} %bitcast.66), calls=%async_computation | async-start | bytes 3670016 | tf_op jit(solution)/shard_map/all_to_all | solution.py:264
  159.0 3.1 %copy-start = (bf16[1,1,1024,3584]{3,2,1,0:T(8,128)(2,1)S(1)}, bf16[1,1,1024,3584]{3,2,1,0:T(8,128)(2,1)}, u32[]{:S(2)}) copy-start(bf16[1,1,1024,3584]{3,2,1,0:T(8,128)(2,1)} %param.8) | copy-start | bytes 22020100
  162.1 1.5 copy-start.7
  163.6 5.8 %copy-start.5 = (bf16[16,32,1792]{2,1,0:T(8,128)(2,1)S(1)}, bf16[16,32,1792]{2,1,0:T(8,128)(2,1)}, u32[]{:S(2)}) copy-start(bf16[16,32,1792]{2,1,0:T(8,128)(2,1)} %copy-done.4) | copy-start | bytes 5505028
  169.4 3.1 %copy-start.1 = (bf16[1,1,1024,3584]{3,2,1,0:T(8,128)(2,1)S(1)}, bf16[1,1,1024,3584]{3,2,1,0:T(8,128)(2,1)}, u32[]{:S(2)}) copy-start(bf16[1,1,1024,3584]{3,2,1,0:T(8,128)(2,1)} %param.8) | copy-start | bytes 22020100
  193.4 3.1 %copy-start.2 = (bf16[1,1,1024,3584]{3,2,1,0:T(8,128)(2,1)S(1)}, bf16[1,1,1024,3584]{3,2,1,0:T(8,128)(2,1)}, u32[]{:S(2)}) copy-start(bf16[1,1,1024,3584]{3,2,1,0:T(8,128)(2,1)} %param.8) | copy-start | bytes 22020100
